TPU v7x, 32 devices: a whole 2x2x4 slice. The times are simulated.
32 devices in a mesh: groups: 2 (over y), row: 4 (over z), col: 2 (over x), rep: 2 (over core).
Axes of the slice: x: 2, y: 2, z: 4, core: 2. Of those that a mesh axis runs over, the one named last changes fastest.
Arguments:
- kernel: float32 [32768, 16384], P(('groups', 'row'), ('col', 'rep')), parts along dimension 0, may hold values from 0 to 2, as said below
- source: float32 [64, 16384], P('groups', 'row'), parts along dimension 0, may hold values from 0.5 to 2, as said below
- target: float32 [64, 16384], P('groups', ('col', 'rep')), parts along dimension 0, may hold values from 0.5 to 2, as said below
Outputs:
- left_scale: float32 [64, 16384], P('groups', 'row'), parts along dimension 0
- right_scale: float32 [64, 16384], P('groups', ('col', 'rep')), parts along dimension 0
- errors: float32 [6, 32], P('groups'), parts along dimension 0
There are 2 independent parts, one for each index of `groups`. A program takes and returns all parts, laid end to end along the dimension named above; each array names one. Nothing has to cross between parts.
Inputs may be any that keep to these rules, and one draw needn't show every extreme that they name: `kernel`: every entry is positive. `source`: every entry is positive. `target`: every entry is positive.
All inputs are finite; a program needn't handle non-finite values.
Results may differ from a plain program's by a relative error of at most 0.0001.
Values sent between devices are 32-bit elements; how exact they have to be, the bound alone decides.
A program may use at most 128 MiB of HBM per device.

v0:
```python
import jax
import jax.numpy as jnp
from jax import lax
from jax.sharding import PartitionSpec as P

N = 16384
ITERS = 3


def local(kernel, source, target):
    columns = kernel.shape[1]
    right_scale = jnp.ones(target.shape, jnp.float32)
    left_scale = source
    share = columns // lax.axis_size("row")
    offset = lax.axis_index("row") * share
    errors = []
    for step in range(ITERS):
        partial_value = lax.dot_general(
            right_scale, kernel, (((1,), (1,)), ((), ())), precision=lax.Precision.HIGHEST
        )
        left_scale = source / lax.psum(partial_value, ("col", "rep"))
        back = jnp.dot(left_scale, kernel, precision=lax.Precision.HIGHEST)
        old_piece = lax.dynamic_slice_in_dim(right_scale, offset, share, 1)
        target_piece = lax.dynamic_slice_in_dim(target, offset, share, 1)
        total_piece = lax.psum_scatter(back, "row", scatter_dimension=1, tiled=True)
        right_scale = lax.all_gather(target_piece / total_piece, "row", axis=1, tiled=True)
        term = jnp.sum(jnp.abs(old_piece * total_piece - target_piece), axis=1) / N
        errors.append(lax.psum(term, ("row", "col", "rep")))
    stacked = jnp.stack(errors)
    return (left_scale, right_scale, stacked)


def solution(mesh):
    return jax.shard_map(
        local,
        mesh=mesh,
        in_specs=(
            P(("groups", "row"), ("col", "rep")),
            P("groups", "row"),
            P("groups", ("col", "rep")),
        ),
        out_specs=(P("groups", "row"), P("groups", ("col", "rep")), P("groups", None)),
        check_vma=False,
    )
```

profile of v0, /device:TPU:0, one launch (start us, length us, event | category | flops | bytes accessed | tf_op | source)
XLA Modules:
  0.0 597.1 jit_solution(12538912805392526422)
XLA Ops:
  7.2 0.0 all-reduce.5.cloned.1.call-start
  7.2 66.4 %fusion.4 = f32[32,4096]{1,0:T(8,128)} fusion(f32[4096,4096]{1,0:T(8,128)} %param.3), kind=kOutput, calls=%fused_computation.4 | convolution fusion | flops 6442450944 | bytes 67633152 | tf_op jit(solution)/shard_map/dot_general | solution.py:18
  73.7 0.0 all-reduce.5.cloned.1.call-update
  73.7 0.3 reduce-scatter.4.cloned.1.call-start
  74.0 36.0 %all-reduce.5.cloned.1.call-done = f32[32,4096]{1,0:T(8,128)} async-done(((f32[32,4096]{1,0:T(8,128)}), f32[32,4096]{1,0:T(8,128)}) %all-reduce.5.cloned.1.call-update) | async-done | bytes 524304 | tf_op jit(solution)/shard_map/psum | solution.py:21
  110.0 44.8 %fusion.2 = f32[32,4096]{1,0:T(8,128)} fusion(f32[4096,4096]{1,0:T(8,128)} %param.3, f32[32,4096]{1,0:T(8,128)S(1)} %copy-done, f32[32,4096]{1,0:T(8,128)} %all-reduce.5.cloned.1.call-done), kind=kOutput, calls=%fused_computation.2 | convolution fusion | flops 6442582016 | bytes 68681728 | tf_op jit(solution)/shard_map/dot_general | solution.py:22
  154.8 0.0 reduce-scatter.4.cloned.1.call-update
  154.9 0.0 all-reduce.7.cloned.1.call-start
  154.9 22.1 %reduce-scatter.4.cloned.1.call-done = f32[32,1024]{1,0:T(8,128)} async-done(((f32[32,4096]{1,0:T(8,128)}), f32[32,1024]{1,0:T(8,128)}) %reduce-scatter.4.cloned.1.call-update) | async-done | bytes 131088 | tf_op jit(solution)/shard_map/reduce_scatter | solution.py:25
  177.0 0.9 dynamic-slice_divide_fusion.2
  177.9 15.7 %all_gather.9 = f32[32,4096]{1,0:T(8,128)S(1)} all-gather(f32[32,1024]{1,0:T(8,128)S(1)} %dynamic-slice_divide_fusion.2), channel_id=1, replica_groups=mesh['groups'=2,'row'=4,'col'=2,'rep'=2] {'row'}, dimensions={1}, use_global_device_ids=true | all-gather | bytes 655360 | tf_op jit(solution)/shard_map/all_gather | solution.py:26
  193.7 66.5 %fusion.7 = f32[32,4096]{1,0:T(8,128)} fusion(f32[32,4096]{1,0:T(8,128)S(1)} %all_gather.9, f32[4096,4096]{1,0:T(8,128)} %param.3), kind=kOutput, calls=%fused_computation.17 | convolution fusion | flops 6442450944 | bytes 68157440 | tf_op jit(solution)/shard_map/dot_general | solution.py:18
  260.2 0.0 all-reduce.7.cloned.1.call-update
  260.2 0.2 reduce-scatter.6.cloned.1.call-start
  260.4 31.8 %all-reduce.7.cloned.1.call-done = f32[32,4096]{1,0:T(8,128)} async-done(((f32[32,4096]{1,0:T(8,128)}), f32[32,4096]{1,0:T(8,128)}) %all-reduce.7.cloned.1.call-update) | async-done | bytes 524304 | tf_op jit(solution)/shard_map/psum | solution.py:21
  292.2 44.8 %fusion = f32[32,4096]{1,0:T(8,128)} fusion(f32[4096,4096]{1,0:T(8,128)} %param.3, f32[32,4096]{1,0:T(8,128)S(1)} %copy-done, f32[32,4096]{1,0:T(8,128)} %all-reduce.7.cloned.1.call-done), kind=kOutput, calls=%fused_computation | convolution fusion | flops 6442582016 | bytes 68681728 | tf_op jit(solution)/shard_map/dot_general | solution.py:22
  337.0 0.0 all-reduce.9.cloned.1.call-start
  337.1 22.0 %reduce-scatter.6.cloned.1.call-done = f32[32,1024]{1,0:T(8,128)} async-done(((f32[32,4096]{1,0:T(8,128)}), f32[32,1024]{1,0:T(8,128)}) %reduce-scatter.6.cloned.1.call-update) | async-done | bytes 131088 | tf_op jit(solution)/shard_map/reduce_scatter | solution.py:25
  359.1 0.9 dynamic-slice_divide_fusion.1
  360.0 15.7 %all_gather.10 = f32[32,4096]{1,0:T(8,128)S(1)} all-gather(f32[32,1024]{1,0:T(8,128)S(1)} %dynamic-slice_divide_fusion.1), channel_id=1, replica_groups=mesh['groups'=2,'row'=4,'col'=2,'rep'=2] {'row'}, dimensions={1}, use_global_device_ids=true | all-gather | bytes 655360 | tf_op jit(solution)/shard_map/all_gather | solution.py:26
  375.7 66.5 %fusion.8 = f32[32,4096]{1,0:T(8,128)} fusion(f32[32,4096]{1,0:T(8,128)S(1)} %all_gather.10, f32[4096,4096]{1,0:T(8,128)} %param.3), kind=kOutput, calls=%fused_computation.18 | convolution fusion | flops 6442450944 | bytes 68157440 | tf_op jit(solution)/shard_map/dot_general | solution.py:18
  442.2 0.0 all-reduce.9.cloned.1.call-update
  442.2 0.3 reduce-scatter.8.cloned.1.call-start
  442.5 31.6 %all-reduce.9.cloned.1.call-done = f32[32,4096]{1,0:T(8,128)} async-done(((f32[32,4096]{1,0:T(8,128)}), f32[32,4096]{1,0:T(8,128)}) %all-reduce.9.cloned.1.call-update) | async-done | bytes 524304 | tf_op jit(solution)/shard_map/psum | solution.py:21
  474.2 1.1 div.31
  475.3 45.0 %fusion.9 = f32[32,4096]{1,0:T(8,128)} fusion(f32[32,4096]{1,0:T(8,128)S(1)} %div.31, f32[4096,4096]{1,0:T(8,128)} %param.3), kind=kOutput, calls=%fused_computation.19 | convolution fusion | flops 6442450944 | bytes 68157440 | tf_op jit(solution)/shard_map/dot_general | solution.py:22
  520.4 22.1 %reduce-scatter.8.cloned.1.call-done = f32[32,1024]{1,0:T(8,128)} async-done(((f32[32,4096]{1,0:T(8,128)}), f32[32,1024]{1,0:T(8,128)}) %reduce-scatter.8.cloned.1.call-update) | async-done | bytes 131088 | tf_op jit(solution)/shard_map/reduce_scatter | solution.py:25
  542.5 1.1 abs_reduce_fusion.2
  543.6 15.3 %all_gather.11 = f32[32,4096]{1,0:T(8,128)S(1)} all-gather(f32[32,1024]{1,0:T(8,128)S(1)} %get-tuple-element.9), channel_id=1, replica_groups=mesh['groups'=2,'row'=4,'col'=2,'rep'=2] {'row'}, dimensions={1}, use_global_device_ids=true | all-gather | bytes 655360 | tf_op jit(solution)/shard_map/all_gather | solution.py:26
  558.9 29.5 %all-reduce = (f32[1,32]{1,0:T(1,128)S(1)}, f32[1,32]{1,0:T(1,128)S(1)}, f32[1,32]{1,0:T(1,128)S(1)}) all-reduce(f32[1,32]{1,0:T(1,128)S(1)} %get-tuple-element.10, f32[1,32]{1,0:T(1,128)S(1)} %get-tuple-element.11, f32[1,32]{1,0:T(1,128)S(1)} %multiply_bitcast_fusion.2), channel_id=1, replica_groups=mesh['groups'=2,'row'=4,'col'=2,'rep'=2] {'row','col','rep'}, use_global_device_ids=true, to_apply=%region_11.0 | all-reduce | flops 96 | bytes 768 | tf_op jit(solution)/shard_map/psum | solution.py:28
  588.4 0.6 pad_maximum_fusion
  589.0 0.8 copy.10
  (14 shorter events, 0.1 us)
Async XLA Ops:
  7.2 102.8 %copy-start = (f32[32,4096]{1,0:T(8,128)S(1)}, f32[32,4096]{1,0:T(8,128)}, u32[]{:S(2)}) copy-start(f32[32,4096]{1,0:T(8,128)} %param.4) | copy-start | bytes 1572868
  7.2 102.8 %all-reduce.5.cloned.1.call-start = ((), (), s32[]{:S(2)}) async-start(), calls=%async_computation.3 | async-start | bytes 1048576 | tf_op jit(solution)/shard_map/psum | solution.py:21
  73.7 103.3 %copy-start.4 = (f32[32,4096]{1,0:T(8,128)S(1)}, f32[32,4096]{1,0:T(8,128)}, u32[]{:S(2)}) copy-start(f32[32,4096]{1,0:T(8,128)} %param.5) | copy-start | bytes 1572868
  73.7 103.3 %reduce-scatter.4.cloned.1.call-start = ((), (), s32[]{:S(2)}) async-start(), calls=%async_computation.4 | async-start | bytes 655360 | tf_op jit(solution)/shard_map/reduce_scatter | solution.py:25
  154.9 137.3 %all-reduce.7.cloned.1.call-start = ((), (), s32[]{:S(2)}) async-start(), calls=%async_computation.5 | async-start | bytes 1048576 | tf_op jit(solution)/shard_map/psum | solution.py:21
  260.2 98.9 %reduce-scatter.6.cloned.1.call-start = ((), (), s32[]{:S(2)}) async-start(), calls=%async_computation.6 | async-start | bytes 655360 | tf_op jit(solution)/shard_map/reduce_scatter | solution.py:25
  337.0 137.1 %all-reduce.9.cloned.1.call-start = ((), (), s32[]{:S(2)}) async-start(), calls=%async_computation.7 | async-start | bytes 1048576 | tf_op jit(solution)/shard_map/psum | solution.py:21
  442.2 100.3 %copy-start.2 = (f32[32,1024]{1,0:T(8,128)S(1)}, f32[32,1024]{1,0:T(8,128)}, u32[]{:S(2)}) copy-start(f32[32,1024]{1,0:T(8,128)} %reduce-scatter.4.cloned.1.call-done) | copy-start | bytes 393220
  442.2 100.3 %copy-start.3 = (f32[32,1024]{1,0:T(8,128)S(1)}, f32[32,1024]{1,0:T(8,128)}, u32[]{:S(2)}) copy-start(f32[32,1024]{1,0:T(8,128)} %reduce-scatter.6.cloned.1.call-done) | copy-start | bytes 393220
  442.2 100.2 %reduce-scatter.8.cloned.1.call-start = ((), (), s32[]{:S(2)}) async-start(), calls=%async_computation.8 | async-start | bytes 655360 | tf_op jit(solution)/shard_map/reduce_scatter | solution.py:25
  475.3 114.5 %copy-start.1 = (f32[32,4096]{1,0:T(8,128)}, f32[32,4096]{1,0:T(8,128)S(1)}, u32[]{:S(2)}) copy-start(f32[32,4096]{1,0:T(8,128)S(1)} %div.31) | copy-start | bytes 1572868
Sparse Core Ops, SparseCore 0:
  73.8 36.1 all-reduce.4
  155.0 21.9 reduce-scatter.3
  260.3 31.8 all-reduce.6
  337.1 21.9 reduce-scatter.5
  442.4 31.7 all-reduce.8
  520.5 21.9 reduce-scatter.7
where the time goes:
time: 606 us; the launch traced here: 597 us
  matrix products  334 us (55%)
  waiting for transfers between devices  166 us (27%)
  blocking collectives  76.2 us (13%)
  between operations  14.6 us (2%)
    dot_general x3, matrix products, local(): lax.dot_general(right_scale, kernel, (((1,), (1,)), ((), ())), precision=...  199 us
    dot_general x3, matrix products, local(): back = jnp.dot(left_scale, kernel, precision=lax.Precision.HIGHEST)  135 us
    psum x3, waiting for transfers between devices, local(): left_scale = source / lax.psum(partial_value, ('col', 'rep'))  99.4 us
    reduce_scatter x3, waiting for transfers between devices, local(): total_piece = lax.psum_scatter(back, 'row', scatter_dimension=1, tiled=True)  66.2 us
    all_gather x3, blocking collectives, local(): lax.all_gather(target_piece / total_piece, 'row', axis=1, tiled=True)  46.8 us
    psum x1, blocking collectives, local(): errors.append(lax.psum(term, ('row', 'col', 'rep')))  29.5 us
  transfers between devices with their start and end apart: 6, of which 6 were waited for; matrix products, arithmetic and copies ran while one was open for 0% of the time, Pallas kernels for 0%

commit v1 on v0

--- a/solution.py
+++ b/solution.py
@@ -18,7 +18,7 @@
         partial_value = lax.dot_general(
             right_scale, kernel, (((1,), (1,)), ((), ())), precision=lax.Precision.HIGHEST
         )
-        left_scale = source / lax.psum(partial_value, ("col", "rep"))
+        left_scale = source / lax.psum(lax.psum(partial_value, axis_name="col"), axis_name="rep")
         back = jnp.dot(left_scale, kernel, precision=lax.Precision.HIGHEST)
         old_piece = lax.dynamic_slice_in_dim(right_scale, offset, share, 1)
         target_piece = lax.dynamic_slice_in_dim(target, offset, share, 1)

time: 606 us -> 657 us (1.084)
  waiting for transfers between devices: 166 us -> 217 us
    psum x3 -> x6, waiting for transfers between devices: 99.4 us -> 148 us  [the longest x3 85.8 us: local(): lax.psum(partial_value, axis_name='col')]
  transfers between devices with their start and end apart: 6 -> 9, of which waited for: 6 -> 9; matrix products, arithmetic and copies ran while one was open for 0% -> 0% of each run, Pallas kernels for 0% -> 0%
where the time goes in v1:
time: 657 us; the launch traced here: 649 us
  matrix products  334 us (51%)
  waiting for transfers between devices  217 us (33%)
  blocking collectives  76.4 us (12%)
  between operations  14.3 us (2%)
    dot_general x3, matrix products, local(): lax.dot_general(right_scale, kernel, (((1,), (1,)), ((), ())), precision=...  199 us
    dot_general x3, matrix products, local(): back = jnp.dot(left_scale, kernel, precision=lax.Precision.HIGHEST)  135 us
    psum x3, waiting for transfers between devices, local(): lax.psum(partial_value, axis_name='col')  85.8 us
    reduce_scatter x3, waiting for transfers between devices, local(): total_piece = lax.psum_scatter(back, 'row', scatter_dimension=1, tiled=True)  69.5 us
    psum x3, waiting for transfers between devices, local(): lax.psum(lax.psum(partial_value, axis_name='col'), axis_name='rep')  61.9 us
    all_gather x3, blocking collectives, local(): lax.all_gather(target_piece / total_piece, 'row', axis=1, tiled=True)  46.9 us
    psum x1, blocking collectives, local(): errors.append(lax.psum(term, ('row', 'col', 'rep')))  29.5 us
  transfers between devices with their start and end apart: 9, of which 9 were waited for; matrix products, arithmetic and copies ran while one was open for 0% of the time, Pallas kernels for 0%

profile of v1, /device:TPU:0, one launch (start us, length us, event | category | flops | bytes accessed | tf_op | source)
XLA Modules:
  0.0 648.8 jit_solution(10131668350359479121)
XLA Ops:
  7.2 66.4 %fusion.4 = f32[32,4096]{1,0:T(8,128)} fusion(f32[4096,4096]{1,0:T(8,128)} %param.3), kind=kOutput, calls=%fused_computation.4 | convolution fusion | flops 6442450944 | bytes 67633152 | tf_op jit(solution)/shard_map/dot_general | solution.py:18
  73.7 31.5 %all-reduce.8.cloned.1.call-done = f32[32,4096]{1,0:T(8,128)} async-done(((f32[32,4096]{1,0:T(8,128)}), f32[32,4096]{1,0:T(8,128)}) %all-reduce.8.cloned.1.call-update) | async-done | bytes 524304 | tf_op jit(solution)/shard_map/psum | solution.py:21
  105.3 0.3 reduce-scatter.4.cloned.1.call-start
  105.5 20.7 %all-reduce.10.cloned.1.call-done = f32[32,4096]{1,0:T(8,128)} async-done(((f32[32,4096]{1,0:T(8,128)}), f32[32,4096]{1,0:T(8,128)}) %all-reduce.10.cloned.1.call-update) | async-done | bytes 524304 | tf_op jit(solution)/shard_map/psum | solution.py:21
  126.2 44.8 %fusion.2 = f32[32,4096]{1,0:T(8,128)} fusion(f32[4096,4096]{1,0:T(8,128)} %param.3, f32[32,4096]{1,0:T(8,128)S(1)} %copy-done, f32[32,4096]{1,0:T(8,128)} %all-reduce.10.cloned.1.call-done), kind=kOutput, calls=%fused_computation.2 | convolution fusion | flops 6442582016 | bytes 68681728 | tf_op jit(solution)/shard_map/dot_general | solution.py:22
  171.1 0.0 all-reduce.12.cloned.1.call-start
  171.1 23.2 %reduce-scatter.4.cloned.1.call-done = f32[32,1024]{1,0:T(8,128)} async-done(((f32[32,4096]{1,0:T(8,128)}), f32[32,1024]{1,0:T(8,128)}) %reduce-scatter.4.cloned.1.call-update) | async-done | bytes 131088 | tf_op jit(solution)/shard_map/reduce_scatter | solution.py:25
  194.3 0.9 dynamic-slice_divide_fusion.2
  195.2 15.9 %all_gather.9 = f32[32,4096]{1,0:T(8,128)S(1)} all-gather(f32[32,1024]{1,0:T(8,128)S(1)} %dynamic-slice_divide_fusion.2), channel_id=1, replica_groups=mesh['groups'=2,'row'=4,'col'=2,'rep'=2] {'row'}, dimensions={1}, use_global_device_ids=true | all-gather | bytes 655360 | tf_op jit(solution)/shard_map/all_gather | solution.py:26
  211.1 66.5 %fusion.7 = f32[32,4096]{1,0:T(8,128)} fusion(f32[32,4096]{1,0:T(8,128)S(1)} %all_gather.9, f32[4096,4096]{1,0:T(8,128)} %param.3), kind=kOutput, calls=%fused_computation.17 | convolution fusion | flops 6442450944 | bytes 68157440 | tf_op jit(solution)/shard_map/dot_general | solution.py:18
  277.6 0.0 all-reduce.14.cloned.1.call-start
  277.6 27.1 %all-reduce.12.cloned.1.call-done = f32[32,4096]{1,0:T(8,128)} async-done(((f32[32,4096]{1,0:T(8,128)}), f32[32,4096]{1,0:T(8,128)}) %all-reduce.12.cloned.1.call-update) | async-done | bytes 524304 | tf_op jit(solution)/shard_map/psum | solution.py:21
  304.8 0.2 reduce-scatter.6.cloned.1.call-start
  305.0 20.6 %all-reduce.14.cloned.1.call-done = f32[32,4096]{1,0:T(8,128)} async-done(((f32[32,4096]{1,0:T(8,128)}), f32[32,4096]{1,0:T(8,128)}) %all-reduce.14.cloned.1.call-update) | async-done | bytes 524304 | tf_op jit(solution)/shard_map/psum | solution.py:21
  325.6 44.8 %fusion = f32[32,4096]{1,0:T(8,128)} fusion(f32[4096,4096]{1,0:T(8,128)} %param.3, f32[32,4096]{1,0:T(8,128)S(1)} %copy-done, f32[32,4096]{1,0:T(8,128)} %all-reduce.14.cloned.1.call-done), kind=kOutput, calls=%fused_computation | convolution fusion | flops 6442582016 | bytes 68681728 | tf_op jit(solution)/shard_map/dot_general | solution.py:22
  370.4 0.0 all-reduce.16.cloned.1.call-start
  370.5 23.2 %reduce-scatter.6.cloned.1.call-done = f32[32,1024]{1,0:T(8,128)} async-done(((f32[32,4096]{1,0:T(8,128)}), f32[32,1024]{1,0:T(8,128)}) %reduce-scatter.6.cloned.1.call-update) | async-done | bytes 131088 | tf_op jit(solution)/shard_map/reduce_scatter | solution.py:25
  393.6 0.9 dynamic-slice_divide_fusion.1
  394.6 15.6 %all_gather.10 = f32[32,4096]{1,0:T(8,128)S(1)} all-gather(f32[32,1024]{1,0:T(8,128)S(1)} %dynamic-slice_divide_fusion.1), channel_id=1, replica_groups=mesh['groups'=2,'row'=4,'col'=2,'rep'=2] {'row'}, dimensions={1}, use_global_device_ids=true | all-gather | bytes 655360 | tf_op jit(solution)/shard_map/all_gather | solution.py:26
  410.2 66.5 %fusion.8 = f32[32,4096]{1,0:T(8,128)} fusion(f32[32,4096]{1,0:T(8,128)S(1)} %all_gather.10, f32[4096,4096]{1,0:T(8,128)} %param.3), kind=kOutput, calls=%fused_computation.18 | convolution fusion | flops 6442450944 | bytes 68157440 | tf_op jit(solution)/shard_map/dot_general | solution.py:18
  476.7 0.0 all-reduce.18.cloned.1.call-start
  476.7 27.2 %all-reduce.16.cloned.1.call-done = f32[32,4096]{1,0:T(8,128)} async-done(((f32[32,4096]{1,0:T(8,128)}), f32[32,4096]{1,0:T(8,128)}) %all-reduce.16.cloned.1.call-update) | async-done | bytes 524304 | tf_op jit(solution)/shard_map/psum | solution.py:21
  504.0 0.3 reduce-scatter.8.cloned.1.call-start
  504.3 20.7 %all-reduce.18.cloned.1.call-done = f32[32,4096]{1,0:T(8,128)} async-done(((f32[32,4096]{1,0:T(8,128)}), f32[32,4096]{1,0:T(8,128)}) %all-reduce.18.cloned.1.call-update) | async-done | bytes 524304 | tf_op jit(solution)/shard_map/psum | solution.py:21
  525.0 1.1 div.31
  526.1 45.0 %fusion.9 = f32[32,4096]{1,0:T(8,128)} fusion(f32[32,4096]{1,0:T(8,128)S(1)} %div.31, f32[4096,4096]{1,0:T(8,128)} %param.3), kind=kOutput, calls=%fused_computation.19 | convolution fusion | flops 6442450944 | bytes 68157440 | tf_op jit(solution)/shard_map/dot_general | solution.py:22
  571.1 23.2 %reduce-scatter.8.cloned.1.call-done = f32[32,1024]{1,0:T(8,128)} async-done(((f32[32,4096]{1,0:T(8,128)}), f32[32,1024]{1,0:T(8,128)}) %reduce-scatter.8.cloned.1.call-update) | async-done | bytes 131088 | tf_op jit(solution)/shard_map/reduce_scatter | solution.py:25
  594.3 1.1 abs_reduce_fusion.2
  595.4 15.5 %all_gather.11 = f32[32,4096]{1,0:T(8,128)S(1)} all-gather(f32[32,1024]{1,0:T(8,128)S(1)} %get-tuple-element.9), channel_id=1, replica_groups=mesh['groups'=2,'row'=4,'col'=2,'rep'=2] {'row'}, dimensions={1}, use_global_device_ids=true | all-gather | bytes 655360 | tf_op jit(solution)/shard_map/all_gather | solution.py:26
  610.9 29.5 %all-reduce = (f32[1,32]{1,0:T(1,128)S(1)}, f32[1,32]{1,0:T(1,128)S(1)}, f32[1,32]{1,0:T(1,128)S(1)}) all-reduce(f32[1,32]{1,0:T(1,128)S(1)} %get-tuple-element.10, f32[1,32]{1,0:T(1,128)S(1)} %get-tuple-element.11, f32[1,32]{1,0:T(1,128)S(1)} %multiply_bitcast_fusion.2), channel_id=1, replica_groups=mesh['groups'=2,'row'=4,'col'=2,'rep'=2] {'row','col','rep'}, use_global_device_ids=true, to_apply=%region_14.0 | all-reduce | flops 96 | bytes 768 | tf_op jit(solution)/shard_map/psum | solution.py:28
  640.4 0.6 pad_maximum_fusion
  641.0 0.8 copy.13
  (23 shorter events, 0.3 us)
Async XLA Ops:
  7.2 119.0 %copy-start = (f32[32,4096]{1,0:T(8,128)S(1)}, f32[32,4096]{1,0:T(8,128)}, u32[]{:S(2)}) copy-start(f32[32,4096]{1,0:T(8,128)} %param.4) | copy-start | bytes 1572868
  7.2 98.1 %all-reduce.8.cloned.1.call-start = ((), (), s32[]{:S(2)}) async-start(), calls=%async_computation.3 | async-start | bytes 1048576 | tf_op jit(solution)/shard_map/psum | solution.py:21
  73.7 120.6 %copy-start.4 = (f32[32,4096]{1,0:T(8,128)S(1)}, f32[32,4096]{1,0:T(8,128)}, u32[]{:S(2)}) copy-start(f32[32,4096]{1,0:T(8,128)} %param.5) | copy-start | bytes 1572868
  73.7 52.5 %all-reduce.10.cloned.1.call-start = ((), (), s32[]{:S(2)}) async-start(), calls=%async_computation.4 | async-start | bytes 1048576 | tf_op jit(solution)/shard_map/psum | solution.py:21
  105.3 89.0 %reduce-scatter.4.cloned.1.call-start = ((), (), s32[]{:S(2)}) async-start(), calls=%async_computation.5 | async-start | bytes 655360 | tf_op jit(solution)/shard_map/reduce_scatter | solution.py:25
  171.1 133.7 %all-reduce.12.cloned.1.call-start = ((), (), s32[]{:S(2)}) async-start(), calls=%async_computation.6 | async-start | bytes 1048576 | tf_op jit(solution)/shard_map/psum | solution.py:21
  277.6 48.0 %all-reduce.14.cloned.1.call-start = ((), (), s32[]{:S(2)}) async-start(), calls=%async_computation.7 | async-start | bytes 1048576 | tf_op jit(solution)/shard_map/psum | solution.py:21
  304.8 88.9 %reduce-scatter.6.cloned.1.call-start = ((), (), s32[]{:S(2)}) async-start(), calls=%async_computation.8 | async-start | bytes 655360 | tf_op jit(solution)/shard_map/reduce_scatter | solution.py:25
  370.4 133.5 %all-reduce.16.cloned.1.call-start = ((), (), s32[]{:S(2)}) async-start(), calls=%async_computation.9 | async-start | bytes 1048576 | tf_op jit(solution)/shard_map/psum | solution.py:21
  476.7 117.7 %copy-start.2 = (f32[32,1024]{1,0:T(8,128)S(1)}, f32[32,1024]{1,0:T(8,128)}, u32[]{:S(2)}) copy-start(f32[32,1024]{1,0:T(8,128)} %reduce-scatter.4.cloned.1.call-done) | copy-start | bytes 393220
  476.7 117.7 %copy-start.3 = (f32[32,1024]{1,0:T(8,128)S(1)}, f32[32,1024]{1,0:T(8,128)}, u32[]{:S(2)}) copy-start(f32[32,1024]{1,0:T(8,128)} %reduce-scatter.6.cloned.1.call-done) | copy-start | bytes 393220
  476.7 48.3 %all-reduce.18.cloned.1.call-start = ((), (), s32[]{:S(2)}) async-start(), calls=%async_computation.10 | async-start | bytes 1048576 | tf_op jit(solution)/shard_map/psum | solution.py:21
  504.0 90.3 %reduce-scatter.8.cloned.1.call-start = ((), (), s32[]{:S(2)}) async-start(), calls=%async_computation.11 | async-start | bytes 655360 | tf_op jit(solution)/shard_map/reduce_scatter | solution.py:25
  526.1 115.7 %copy-start.1 = (f32[32,4096]{1,0:T(8,128)}, f32[32,4096]{1,0:T(8,128)S(1)}, u32[]{:S(2)}) copy-start(f32[32,4096]{1,0:T(8,128)S(1)} %div.31) | copy-start | bytes 1572868
Sparse Core Ops, SparseCore 0:
  73.8 31.3 all-reduce.7
  107.6 18.5 all-reduce.9
  171.2 23.0 reduce-scatter.3
  277.7 26.9 all-reduce.11
  306.9 18.5 all-reduce.13
  370.6 23.0 reduce-scatter.5
  476.8 27.1 all-reduce.15
  506.3 18.5 all-reduce.17
  571.3 23.0 reduce-scatter.7
